TPU v7x, 256 devices: a whole 4x4x8 slice. The times are simulated.
256 devices in a mesh: sec: 32 (over z_hi, y, core), narrow: 8 (over x, z_lo).
Axes of the slice: x: 4, y: 4, z: 8 (z_hi: 4, z_lo: 2; z = z_hi * 2 + z_lo), core: 2. Of those that a mesh axis runs over, the one named last changes fastest.
Arguments:
- tokens: bfloat16 [4096, 2048], P('sec'), may hold values from -8 to 8
- attn_gain: float32 [2048], replicated, may hold values from 0.5 to 1.5
- w_query: bfloat16 [2048, 4096], P(None, 'narrow'), may hold values from -0.125 to 0.125
- w_key: bfloat16 [2048, 512], P(None, 'narrow'), may hold values from -0.125 to 0.125
- w_value: bfloat16 [2048, 512], P(None, 'narrow'), may hold values from -0.125 to 0.125
- query_gain: float32 [128], replicated, may hold values from 0.6 to 6
- key_gain: float32 [128], replicated, may hold values from 0.6 to 6
- w_out: bfloat16 [4096, 2048], P('narrow'), may hold values from -0.09375 to 0.09375
- moe_gain: float32 [2048], replicated, may hold values from 0.5 to 1.5
- expert_ids: int32 [4096, 8], P('sec'), may hold values from 0 to 127, all different within a row; in each aligned block of 16 rows (0 to 15, 16 to 31, ...) at most 2 rows name the same one
- expert_weights: float32 [4096, 8], P('sec'), may hold values from 0.05 to 1
- w_gate: bfloat16 [128, 2048, 768], P('sec', None, 'narrow'), may hold values from -0.125 to 0.125
- w_up: bfloat16 [128, 2048, 768], P('sec', None, 'narrow'), may hold values from -0.125 to 0.125
- w_down: bfloat16 [128, 768, 2048], P('sec', 'narrow'), may hold values from -0.21875 to 0.21875
Outputs:
- layer_out: bfloat16 [4096, 2048], P(('sec', 'narrow'))
Inputs may be any that keep to these rules, and one draw needn't show every extreme that they name: `expert_ids`: each row names 8 different experts. In each aligned block of 16 rows no expert is named by more than 2 rows, a bound that some block reaches.
All inputs are finite; a program needn't handle non-finite values.
Results may differ from a plain program's by a relative error of at most 0.009.
Values may be sent and summed in bfloat16 or wider, within the bound.
No kernel may reach another device: no remote copies, remote signals or barrier semaphores. Data moves between devices by JAX's collectives and lax.ppermute only.
A program may use at most 128 MiB of HBM per device.

v0:
```python
import math
import jax
import jax.numpy as jnp
from jax import lax
from jax.sharding import Mesh
from jax.sharding import PartitionSpec as P

D = 2048
HEADS = 32
KV_HEADS = 4
HEAD = 128
TOPK = 8
NARROW = ("narrow_0", "narrow_1")
SEC_NARROW = ("sec", "narrow_0", "narrow_1")
norm_eps = 1e-06


def gather_turned(arrays, axis, dims):
    turned = [jnp.moveaxis(a, dim, 0) for a, dim in zip(arrays, dims)]
    both = jnp.concatenate([t.reshape(len(t), -1) for t in turned], axis=1)
    whole, at, finished = (lax.all_gather(both, axis, axis=0, tiled=True), 0, [])
    for t, dim in zip(turned, dims):
        slab = whole[:, at : at + t[0].size].reshape(-1, *t.shape[1:])
        finished.append(jnp.moveaxis(slab, 0, dim))
        at += t[0].size
    return tuple(finished)


def sent_together(arrays, axis, dim, along):
    ends, at = ([], 0)
    for a in arrays[:-1]:
        at += a.shape[along]
        ends.append(at)
    both = jnp.concatenate(arrays, axis=along)
    return tuple(jnp.split(lax.all_gather(both, axis, axis=dim, tiled=True), ends, axis=along))


def in_blocks(x, dim, peers):
    shape = x.shape
    blocks = x.reshape(*shape[:dim], peers, shape[dim] // peers, *shape[dim + 1 :])
    return jnp.moveaxis(blocks, dim, 0)


def sum_at_owner(x, axis, dim):
    peers = lax.axis_size(axis)
    blocks = lax.all_to_all(in_blocks(x, dim, peers), axis, 0, 0, tiled=True)
    return jnp.sum(blocks.astype(jnp.float32), axis=0)


def sum_by_axis(terms, axes):
    running = terms.astype(jnp.bfloat16)
    for axis in axes:
        running = lax.psum_scatter(running, axis, scatter_dimension=0, tiled=True)
    return running.astype(jnp.float32)


def rms_norm(inputs, gain):
    widened = inputs.astype(jnp.float32)
    return (
        widened * lax.rsqrt(jnp.mean(widened * widened, axis=-1, keepdims=True) + norm_eps) * gain
    )


def rotate(inputs, positions):
    half_size = inputs.shape[-1] // 2
    inverse = jnp.exp(
        -jnp.log(1000000.0) * jnp.arange(half_size, dtype=jnp.float32) * 2.0 / inputs.shape[-1]
    )
    angles = positions.astype(jnp.float32)[:, None] * inverse[None, :]
    cosine = jnp.cos(angles)[:, None, :]
    sine = jnp.sin(angles)[:, None, :]
    leading = inputs[..., :half_size]
    trailing = inputs[..., half_size:]
    return jnp.concatenate(
        [leading * cosine - trailing * sine, trailing * cosine + leading * sine], axis=-1
    )


def slot_numbers(flat_ids, experts_all):
    onehot = (
        flat_ids[:, :, None] == jnp.arange(experts_all, dtype=jnp.int32)[None, None, :]
    ).astype(jnp.int32)
    earlier = jnp.cumsum(onehot, axis=1) - onehot
    return jnp.sum(earlier * onehot, axis=-1)


def head_columns(whole, kv_start, kv_here):
    width = whole.shape[0]
    strided = whole.reshape(width, HEAD, KV_HEADS)
    picked = lax.dynamic_slice_in_dim(strided, kv_start, kv_here, 2)
    return jnp.transpose(picked, (0, 2, 1)).reshape(width, kv_here * HEAD)


def on_device(
    tokens,
    attn_gain,
    w_query,
    w_key,
    w_value,
    query_gain,
    key_gain,
    w_out,
    moe_gain,
    expert_ids,
    expert_weights,
    w_gate,
    w_up,
    w_down,
):
    sec_count = lax.axis_size("sec")
    narrow_count = lax.axis_size(NARROW)
    sec_index = lax.axis_index("sec")
    narrow_index = lax.axis_index(NARROW)
    local_rows = tokens.shape[0]
    share_rows = local_rows // narrow_count
    expert_here = w_gate.shape[0]
    experts_all = expert_here * sec_count
    capacity = min(share_rows, max(2, 5 * share_rows * TOPK // (2 * experts_all)))
    heads_here = w_query.shape[1] // HEAD
    group_size = HEADS // KV_HEADS
    kv_here = max(1, heads_here // group_size)
    per_key_head = heads_here // kv_here
    kv_start = narrow_index * heads_here // group_size
    scale = 1.0 / math.sqrt(HEAD)
    positions = sec_index * local_rows + jnp.arange(local_rows, dtype=jnp.int32)
    last_position = sec_index * local_rows + local_rows - 1
    normed = rms_norm(tokens, attn_gain).astype(jnp.bfloat16)
    query = jnp.dot(normed, w_query, preferred_element_type=jnp.float32).reshape(
        local_rows, heads_here, HEAD
    )
    query = rotate(rms_norm(query, query_gain), positions).astype(jnp.bfloat16)
    key_whole, value_whole = gather_turned((w_key, w_value), NARROW, (1, 1))
    key_columns = head_columns(key_whole, kv_start, kv_here)
    value_columns = head_columns(value_whole, kv_start, kv_here)
    keys = jnp.dot(normed, key_columns, preferred_element_type=jnp.float32).reshape(
        local_rows, kv_here, HEAD
    )
    keys = (
        rotate(rms_norm(keys, key_gain), positions)
        .astype(jnp.bfloat16)
        .reshape(local_rows, kv_here * HEAD)
    )
    values = jnp.dot(normed, value_columns, preferred_element_type=jnp.float32).astype(jnp.bfloat16)
    grouped = query.reshape(local_rows, kv_here, per_key_head, HEAD)

    def update(state, block_keys, block_values, block_start):
        peak, total, accum = state
        width = block_keys.shape[0]
        scores = (
            jnp.einsum("tcgd,jcd->cgtj", grouped, block_keys, preferred_element_type=jnp.float32)
            * scale
        )
        key_positions = block_start + jnp.arange(width, dtype=jnp.int32)
        allowed = key_positions[None, :] <= positions[:, None]
        scores = jnp.where(allowed, scores, -1e30)
        new_peak = jnp.maximum(peak, jnp.max(scores, axis=-1))
        probs = jnp.where(allowed, jnp.exp(scores - new_peak[..., None]), 0.0)
        factor = jnp.exp(peak - new_peak)
        total = total * factor + jnp.sum(probs, axis=-1)
        accum = accum * factor[..., None] + jnp.einsum(
            "cgtj,jcd->cgtd",
            probs.astype(jnp.bfloat16),
            block_values,
            preferred_element_type=jnp.float32,
        )
        return (new_peak, total, accum)

    start_state = (
        jnp.full((kv_here, per_key_head, local_rows), -1e30, jnp.float32),
        jnp.zeros((kv_here, per_key_head, local_rows), jnp.float32),
        jnp.zeros((kv_here, per_key_head, local_rows, HEAD), jnp.float32),
    )
    carry = start_state
    key_piece, value_piece = sent_together((keys, values), "sec", 0, 1)
    length = key_piece.shape[0]
    width = math.gcd(length, 512)
    blocks = length // width
    key_blocks = key_piece.reshape(blocks, width, kv_here, HEAD)
    value_blocks = value_piece.reshape(blocks, width, kv_here, HEAD)

    def advance(state, inputs):
        block_keys, block_values, number = inputs
        block_start = number * width
        state = lax.cond(
            block_start <= last_position,
            lambda inner: update(inner, block_keys, block_values, block_start),
            lambda inner: inner,
            state,
        )
        return (state, None)

    carry, _ = lax.scan(
        advance, carry, (key_blocks, value_blocks, jnp.arange(blocks, dtype=jnp.int32))
    )
    peak, total, accum = carry
    attended = (
        jnp.transpose(accum / total[..., None], (2, 0, 1, 3))
        .reshape(local_rows, heads_here * HEAD)
        .astype(jnp.bfloat16)
    )
    own_offset = narrow_index * share_rows
    mixed = sum_at_owner(
        jnp.dot(attended, w_out, preferred_element_type=jnp.float32).astype(jnp.bfloat16), NARROW, 0
    )
    own_tokens = lax.dynamic_slice_in_dim(tokens, own_offset, share_rows, 0)
    carried_mine = (own_tokens.astype(jnp.float32) + mixed).astype(jnp.bfloat16)
    send_ids = lax.dynamic_slice_in_dim(expert_ids, own_offset, share_rows, 0)
    send_rows = rms_norm(carried_mine, moe_gain).astype(jnp.bfloat16)
    blocks_sent = 1

    def place(flat_ids, slots):
        return (flat_ids % expert_here * sec_count + flat_ids // expert_here) * capacity + slots

    out_rows = expert_here * sec_count * capacity
    flat_ids = send_ids.reshape(blocks_sent, share_rows * TOPK)
    slots = slot_numbers(flat_ids, experts_all)
    block_index = jnp.arange(blocks_sent, dtype=jnp.int32)[:, None]
    targets = block_index * out_rows + place(flat_ids, slots)
    sources = (
        block_index * share_rows + jnp.arange(share_rows * TOPK, dtype=jnp.int32)[None, :] // TOPK
    )
    table = (
        jnp.full((blocks_sent * out_rows,), blocks_sent * share_rows, jnp.int32)
        .at[targets.reshape(-1)]
        .set(sources.reshape(-1))
    )
    padded = jnp.concatenate([send_rows, jnp.zeros((1, D), jnp.bfloat16)], axis=0)
    outgoing = padded[table].reshape(blocks_sent, expert_here, sec_count, capacity, D)
    arrived = lax.all_to_all(outgoing, "sec", split_axis=2, concat_axis=2, tiled=True)
    piece = lax.all_gather(arrived, NARROW, axis=0, tiled=True)
    count = piece.shape[0]
    rows_in = piece.reshape(count, expert_here, sec_count * capacity, D)
    gate_value = jnp.einsum("berd,edf->berf", rows_in, w_gate, preferred_element_type=jnp.float32)
    up_value = jnp.einsum("berd,edf->berf", rows_in, w_up, preferred_element_type=jnp.float32)
    active = (jax.nn.silu(gate_value) * up_value).astype(jnp.bfloat16)
    number = out_rows * lax.axis_size(NARROW) // out_rows
    expert_total = sum_by_axis(
        jnp.einsum("berf,efd->berd", active, w_down, preferred_element_type=jnp.float32).reshape(
            out_rows * lax.axis_size(NARROW), D
        ),
        NARROW,
    ).astype(jnp.bfloat16)
    returned = lax.all_to_all(
        expert_total.reshape(1, expert_here, sec_count, capacity, D),
        "sec",
        split_axis=2,
        concat_axis=2,
        tiled=True,
    ).reshape(out_rows, D)
    own_ids = lax.dynamic_slice_in_dim(expert_ids, own_offset, share_rows, 0).reshape(
        1, share_rows * TOPK
    )
    own_slots = slot_numbers(own_ids, experts_all)
    picks = place(own_ids, own_slots).reshape(-1)
    gathered = returned[picks].reshape(share_rows, TOPK, D)
    own_weights = lax.dynamic_slice_in_dim(expert_weights, own_offset, share_rows, 0)
    gates = own_weights / jnp.sum(own_weights, axis=-1, keepdims=True)
    mixture = jnp.sum(gates[:, :, None] * gathered.astype(jnp.float32), axis=1)
    return (carried_mine.astype(jnp.float32) + mixture).astype(jnp.bfloat16)


def solution(mesh):
    split = Mesh(mesh.devices.reshape(mesh.shape["sec"], 4, 2), ("sec", "narrow_0", "narrow_1"))
    in_specs = (
        P("sec", None),
        P(),
        P(None, NARROW),
        P(None, NARROW),
        P(None, NARROW),
        P(),
        P(),
        P(NARROW, None),
        P(),
        P("sec", None),
        P("sec", None),
        P("sec", None, NARROW),
        P("sec", None, NARROW),
        P("sec", NARROW, None),
    )
    out_specs = P(SEC_NARROW, None)
    return jax.shard_map(
        on_device, mesh=split, in_specs=in_specs, out_specs=out_specs, check_vma=False
    )
```

profile of v0, /device:TPU:32, one launch (start us, length us, event | category | flops | bytes accessed | tf_op | source)
XLA Modules:
  0.0 678.0 jit_solution(6871199354798693213)
XLA Ops:
  6.5 2.0 pad_maximum_fusion
  8.7 1.2 fusion.38
  9.9 94.0 %all-gather.4.cloned.1.call-done = bf16[512,4096]{1,0:T(8,128)(2,1)} async-done(((bf16[64,4096]{1,0:T(8,128)(2,1)}), bf16[512,4096]{1,0:T(8,128)(2,1)}) %all-gather.4.cloned.1.call-update) | async-done | bytes 4194320 | tf_op jit(solution)/shard_map/all_gather | solution.py:21
  103.9 4.8 slice_bitcast_fusion.1
  108.7 4.1 reshape.600
  112.8 4.1 reshape.601
  116.9 5.4 constant_dynamic-slice_fusion.1
  122.3 3.5 copy.62
  125.8 1.6 multiply_reduce_fusion.1
  127.5 1.9 copy.63
  129.3 1.6 convolution_convert_fusion.1
  131.3 0.6 pad_maximum_fusion.2
  132.3 2.3 fusion.68
  135.7 51.2 %all-gather.6.cloned.1.call-done = bf16[4096,256]{0,1:T(8,128)(2,1)} async-done(((bf16[128,256]{0,1:T(8,128)(2,1)}), bf16[4096,256]{0,1:T(8,128)(2,1)}) %all-gather.6.cloned.1.call-update) | async-done | bytes 2097168 | tf_op jit(solution)/shard_map/all_gather | solution.py:35
  186.9 2.7 fusion.73
  189.6 2.3 copy.81
  191.9 1.3 copy.82
  193.3 13.3 %while.15 = (s32[]{:T(128)}, f32[1,4,128]{2,1,0:T(4,128)S(1)}, f32[1,4,128]{2,1,0:T(4,128)S(1)}, f32[1,4,128,128]{3,2,1,0:T(8,128)S(1)}, s32[8]{0:T(128)S(1)}, /...) while((s32[]{:T(128)}, f32[1,4,128]{2,1,0:T(4,128)S(1)}, ...), condition=%wide.region_8.9_spmd.clone, body=%wide.region_3.8_spmd.clone.sunk | while | flops 136775808 | bytes 4365611 | solution.py:192
  194.5 3.0 conditional.3
  194.7 1.2 fusion.72
  196.2 1.4 fusion.4
  200.2 0.6 dynamic_slice.61
  206.8 1.3 convolution_convert_fusion
  208.1 6.7 all-to-all-start
  215.3 1.0 scatter_custom_fusion
  216.3 7.8 %all-to-all-done = bf16[8,16,2048]{2,1,0:T(8,128)(2,1)S(1)} async-done(((bf16[8,16,2048]{2,1,0:T(8,128)(2,1)}), bf16[8,16,2048]{2,1,0:T(8,128)(2,1)S(1)}, u32[]{:S(2)}, u32[]{:S(2)}) %all-to-all-start) | async-done | bytes 524320 | tf_op jit(solution)/shard_map/all_to_all | solution.py:46
  224.2 1.0 fusion.46
  225.3 1.4 gather_fusion
  226.7 0.7 reshape.607
  227.4 1.1 copy.72
  228.5 52.3 %all_to_all.15 = bf16[1,4,32,2,2048]{4,3,0,1,2:T(2,128)(2,1)} all-to-all(bf16[1,4,32,2,2048]{4,3,0,1,2:T(2,128)(2,1)S(1)} %copy.72), channel_id=1, replica_groups=mesh['sec'=32,'narrow_0'=4,'narrow_1'=2] {'sec'}, dimensions={2} | all-to-all | bytes 2097152 | tf_op jit(solution)/shard_map/all_to_all | solution.py:229
  281.0 169.5 %all-gather.8.cloned.1.call-done = bf16[8,4,32,2,2048]{4,3,0,1,2:T(2,128)(2,1)} async-done(((bf16[1,4,32,2,2048]{4,3,0,1,2:T(2,128)(2,1)}), bf16[8,4,32,2,2048]{4,3,0,1,2:T(2,128)(2,1)}) %all-gather.8.cloned.1.call-update) | async-done | bytes 8388624 | tf_op jit(solution)/shard_map/all_gather | solution.py:230
  450.5 8.2 %copy.73 = bf16[8,4,32,2,2048]{4,3,2,0,1:T(2,128)(2,1)} copy(bf16[8,4,32,2,2048]{4,3,0,1,2:T(2,128)(2,1)} %all-gather.8.cloned.1.call-done) | data formatting | bytes 16777216 | tf_op jit(solution)/shard_map/all_gather | solution.py:230
  458.7 13.1 %reshape.608 = bf16[8,4,64,2048]{3,2,0,1:T(8,128)(2,1)} reshape(bf16[8,4,32,2,2048]{4,3,2,0,1:T(2,128)(2,1)} %copy.73) | data formatting | bytes 16777216 | tf_op jit(solution)/shard_map/reshape | solution.py:232
  471.8 6.1 fusion.26
  477.9 12.0 %convert_bitcast_fusion = bf16[8,4,64,2048]{3,2,0,1:T(8,128)(2,1)} fusion(bf16[4,96,2048]{2,1,0:T(8,128)(2,1)} %param.31, bf16[8,4,64,2048]{3,2,0,1:T(8,128)(2,1)} %reshape.608, bf16[4,2048,96]{1,2,0:T(8,128)(2,1)} %param.30, f32[8,4,64,96]{3,2,0,1:T(8,128)S(1)} %fusion.26), kind=kOutput, calls=%fused_computation.31 | convolution fusion | flops 1615986688 | bytes 20709376 | tf_op jit(solution)/shard_map/berf,efd->berd/dot_general | solution.py:238
  489.9 8.3 %copy.74 = bf16[8,4,64,2048]{3,2,1,0:T(8,128)(2,1)} copy(bf16[8,4,64,2048]{3,2,0,1:T(8,128)(2,1)} %convert_bitcast_fusion) | data formatting | bytes 16777216 | tf_op jit(solution)/shard_map/convert_element_type | solution.py:51
  498.2 84.2 %reduce-scatter.3.cloned.1.call-done = bf16[512,2048]{1,0:T(8,128)(2,1)} async-done(((bf16[2048,2048]{1,0:T(8,128)(2,1)}), bf16[512,2048]{1,0:T(8,128)(2,1)}) %reduce-scatter.3.cloned.1.call-update) | async-done | bytes 2097168 | tf_op jit(solution)/shard_map/reduce_scatter | solution.py:53
  582.5 37.9 %reduce-scatter.5.cloned.1.call-done = bf16[256,2048]{1,0:T(8,128)(2,1)} async-done(((bf16[512,2048]{1,0:T(8,128)(2,1)}), bf16[256,2048]{1,0:T(8,128)(2,1)}) %reduce-scatter.5.cloned.1.call-update) | async-done | bytes 1048592 | tf_op jit(solution)/shard_map/reduce_scatter | solution.py:53
  620.4 1.7 reshape.609
  622.2 2.1 copy.75
  624.3 10.1 %all-to-all-start.2 = ((bf16[1,4,32,2,2048]{4,3,1,0,2:T(2,128)(2,1)}), bf16[1,4,32,2,2048]{4,3,1,0,2:T(2,128)(2,1)S(1)}, u32[]{:S(2)}, u32[]{:S(2)}) async-start(bf16[1,4,32,2,2048]{4,3,1,0,2:T(2,128)(2,1)} %copy.75), calls=%async_computation.4 | async-start | bytes 2097152 | tf_op jit(solution)/shard_map/all_to_all | solution.py:243
  634.6 29.6 %all-to-all-done.2 = bf16[1,4,32,2,2048]{4,3,1,0,2:T(2,128)(2,1)S(1)} async-done(((bf16[1,4,32,2,2048]{4,3,1,0,2:T(2,128)(2,1)}), bf16[1,4,32,2,2048]{4,3,1,0,2:T(2,128)(2,1)S(1)}, u32[]{:S(2)}, u32[]{:S(2)}) %all-to-all-start.2) | async-done | bytes 1048608 | tf_op jit(solution)/shard_map/all_to_all | solution.py:243
  664.2 1.8 copy.76
  666.0 1.6 reshape.610
  667.6 1.7 gather_fusion.1
  669.4 1.5 fusion.41
  670.9 0.6 fusion.49
  (94 shorter events, 7.8 us)
Async XLA Ops:
  6.5 200.3 %copy-start = (bf16[512,2048]{1,0:T(8,128)(2,1)S(1)}, bf16[512,2048]{1,0:T(8,128)(2,1)}, u32[]{:S(2)}) copy-start(bf16[512,2048]{1,0:T(8,128)(2,1)} %param.25) | copy-start | bytes 6291460
  6.5 97.3 %all-gather.4.cloned.1.call-start = ((), (), s32[]{:S(2)}) async-start(), calls=%async_computation.5 | async-start | bytes 4718592 | tf_op jit(solution)/shard_map/all_gather | solution.py:21
  8.6 178.3 %all-gather.6.cloned.1.call-start = ((), (), s32[]{:S(2)}) async-start(), calls=%async_computation.6 | async-start | bytes 2162688 | tf_op jit(solution)/shard_map/all_gather | solution.py:35
  116.9 8.9 %copy-start.3 = (f32[2048]{0:T(1024)S(1)}, f32[2048]{0:T(1024)}, u32[]{:S(2)}) copy-start(f32[2048]{0:T(1024)} %param.19) | copy-start | bytes 24580
  125.8 5.1 copy-start.6
  125.8 6.1 copy-start.5
  131.3 4.0 copy-start.7
  206.8 18.4 %copy-start.4 = (f32[2048]{0:T(1024)S(1)}, f32[2048]{0:T(1024)}, u32[]{:S(2)}) copy-start(f32[2048]{0:T(1024)} %param.26) | copy-start | bytes 24580
  208.1 16.1 %all-to-all-start = ((bf16[8,16,2048]{2,1,0:T(8,128)(2,1)}), bf16[8,16,2048]{2,1,0:T(8,128)(2,1)S(1)}, u32[]{:S(2)}, u32[]{:S(2)}) async-start(bf16[8,16,2048]{2,1,0:T(8,128)(2,1)} %bitcast.29), calls=%async_computation | async-start | bytes 1048576 | tf_op jit(solution)/shard_map/all_to_all | solution.py:46
  214.8 235.7 %all-gather.8.cloned.1.call-start = ((), (), s32[]{:S(2)}) async-start(), calls=%async_computation.7 | async-start | bytes 9437184 | tf_op jit(solution)/shard_map/all_gather | solution.py:230
  280.8 301.7 %reduce-scatter.3.cloned.1.call-start = ((), (), s32[]{:S(2)}) async-start(), calls=%async_computation.8 | async-start | bytes 10485760 | tf_op jit(solution)/shard_map/reduce_scatter | solution.py:53
  498.2 122.2 %reduce-scatter.5.cloned.1.call-start = ((), (), s32[]{:S(2)}) async-start(), calls=%async_computation.9 | async-start | bytes 3145728 | tf_op jit(solution)/shard_map/reduce_scatter | solution.py:53
  622.1 12.2 %copy-start.2 = (f32[128,8]{0,1:T(8,128)S(1)}, f32[128,8]{0,1:T(8,128)}, u32[]{:S(2)}) copy-start(f32[128,8]{0,1:T(8,128)} %param.28) | copy-start | bytes 12292
  624.3 39.9 %all-to-all-start.2 = ((bf16[1,4,32,2,2048]{4,3,1,0,2:T(2,128)(2,1)}), bf16[1,4,32,2,2048]{4,3,1,0,2:T(2,128)(2,1)S(1)}, u32[]{:S(2)}, u32[]{:S(2)}) async-start(bf16[1,4,32,2,2048]{4,3,1,0,2:T(2,128)(2,1)} %copy.75), calls=%async_computation.4 | async-start | bytes 2097152 | tf_op jit(solution)/shard_map/all_to_all | solution.py:243
  666.0 5.5 copy-start.1
Sparse Core Ops, SparseCore 0:
  9.1 94.7 all-gather.3
  132.0 54.8 all-gather.5
  280.9 169.5 all-gather.7
  498.3 84.1 reduce-scatter.2
  584.8 35.5 reduce-scatter.4
where the time goes:
time: 680 us; the launch traced here: 678 us
  waiting for transfers between devices  474 us (70%)
  local copies, waits for them, and re-layouts  78.3 us (12%)
  blocking collectives  52.3 us (8%)
  matrix products  27.4 us (4%)
  starting transfers between devices  17.1 us (3%)
  between operations  13.5 us (2%)
  other arithmetic  9.42 us (1%)
    all_gather x1, waiting for transfers between devices, on_device(): piece = lax.all_gather(arrived, NARROW, axis=0, tiled=True)  169 us
    reduce_scatter x2, waiting for transfers between devices, sum_by_axis(): running = lax.psum_scatter(running, axis, scatter_dimension=0, tiled=True)  122 us
    all_gather x1, waiting for transfers between devices, gather_turned(): lax.all_gather(both, axis, axis=0, tiled=True)  94 us
    all_to_all x1, blocking collectives, on_device(): lax.all_to_all(outgoing, 'sec', split_axis=2, concat_axis=2, tiled=True)  52.3 us
    all_gather x1, waiting for transfers between devices, sent_together(): lax.all_gather(both, axis, axis=dim, tiled=True)  51.2 us
    all_to_all x1, waiting for transfers between devices, on_device(): lax.all_to_all(expert_total.reshape(1, expert_here, sec_count, capacity,...  29.6 us
  transfers between devices with their start and end apart: 7, of which 7 were waited for; matrix products, arithmetic and copies ran while one was open for 1% of the time, Pallas kernels for 0%

commit v1 on v0

--- a/solution.py
+++ b/solution.py
@@ -227,7 +227,10 @@
     padded = jnp.concatenate([send_rows, jnp.zeros((1, D), jnp.bfloat16)], axis=0)
     outgoing = padded[table].reshape(blocks_sent, expert_here, sec_count, capacity, D)
     arrived = lax.all_to_all(outgoing, "sec", split_axis=2, concat_axis=2, tiled=True)
-    piece = lax.all_gather(arrived, NARROW, axis=0, tiled=True)
+    size = lax.axis_size(NARROW)
+    pieces = jnp.stack([arrived for _ in range(size)])
+    pieces = lax.all_to_all(pieces, NARROW, split_axis=0, concat_axis=0)
+    piece = jnp.concatenate(pieces, axis=0)
     count = piece.shape[0]
     rows_in = piece.reshape(count, expert_here, sec_count * capacity, D)
     gate_value = jnp.einsum("berd,edf->berf", rows_in, w_gate, preferred_element_type=jnp.float32)

time: 680 us -> 605 us (0.89)
  waiting for transfers between devices: 474 us -> 299 us
  blocking collectives: 52.3 us -> 155 us
    all_gather x1 -> x0, waiting for transfers between devices: 169 us -> none  [on_device(): piece = lax.all_gather(arrived, NARROW, axis=0, tiled=True)]
    all_to_all x0 -> x1, blocking collectives: none -> 103 us  [on_device(): pieces = lax.all_to_all(pieces, NARROW, split_axis=0, concat_axis=0)]
    another operation x0 -> x2, local copies, waits for them, and re-layouts: none -> 18.9 us  [the longest x1 13.2 us: on_device(): rows_in = piece.reshape(count, expert_here, sec_count * capacity, D)]
    reshape x1 -> x0, local copies, waits for them, and re-layouts: 13.1 us -> none  [on_device(): rows_in = piece.reshape(count, expert_here, sec_count * capacity, D)]
    all_gather x1 -> x0, local copies, waits for them, and re-layouts: 8.16 us -> none  [on_device(): piece = lax.all_gather(arrived, NARROW, axis=0, tiled=True)]
  transfers between devices with their start and end apart: 7 -> 6, of which waited for: 7 -> 6; matrix products, arithmetic and copies ran while one was open for 1% -> 1% of each run, Pallas kernels for 0% -> 0%
where the time goes in v1:
time: 605 us; the launch traced here: 603 us
  waiting for transfers between devices  299 us (49%)
  blocking collectives  155 us (26%)
  local copies, waits for them, and re-layouts  76.8 us (13%)
  matrix products  27 us (4%)
  starting transfers between devices  16.9 us (3%)
  between operations  13.5 us (2%)
  other arithmetic  9.43 us (2%)
    reduce_scatter x2, waiting for transfers between devices, sum_by_axis(): running = lax.psum_scatter(running, axis, scatter_dimension=0, tiled=True)  116 us
    all_to_all x1, blocking collectives, on_device(): pieces = lax.all_to_all(pieces, NARROW, split_axis=0, concat_axis=0)  103 us
    all_gather x1, waiting for transfers between devices, gather_turned(): lax.all_gather(both, axis, axis=0, tiled=True)  94 us
    all_to_all x1, blocking collectives, on_device(): lax.all_to_all(outgoing, 'sec', split_axis=2, concat_axis=2, tiled=True)  52.1 us
    all_gather x1, waiting for transfers between devices, sent_together(): lax.all_gather(both, axis, axis=dim, tiled=True)  51.2 us
    all_to_all x1, waiting for transfers between devices, on_device(): lax.all_to_all(expert_total.reshape(1, expert_here, sec_count, capacity,...  29.6 us
    another operation x1, local copies, waits for them, and re-layouts, on_device(): rows_in = piece.reshape(count, expert_here, sec_count * capacity, D)  13.2 us
  transfers between devices with their start and end apart: 6, of which 6 were waited for; matrix products, arithmetic and copies ran while one was open for 1% of the time, Pallas kernels for 0%

profile of v1, /device:TPU:32, one launch (start us, length us, event | category | flops | bytes accessed | tf_op | source)
XLA Modules:
  0.0 603.2 jit_solution(1720929058779982423)
XLA Ops:
  6.5 2.0 pad_maximum_fusion
  8.7 1.2 fusion.48
  9.9 94.0 %all-gather.3.cloned.1.call-done = bf16[512,4096]{1,0:T(8,128)(2,1)} async-done(((bf16[64,4096]{1,0:T(8,128)(2,1)}), bf16[512,4096]{1,0:T(8,128)(2,1)}) %all-gather.3.cloned.1.call-update) | async-done | bytes 4194320 | tf_op jit(solution)/shard_map/all_gather | solution.py:21
  103.9 4.8 slice_bitcast_fusion.1
  108.7 4.1 reshape.600
  112.8 4.1 reshape.601
  116.9 5.4 constant_dynamic-slice_fusion.1
  122.3 3.5 copy.60
  125.8 1.6 multiply_reduce_fusion.1
  127.5 1.9 copy.61
  129.4 1.6 convolution_convert_fusion.1
  131.3 0.6 pad_maximum_fusion.2
  132.3 2.3 fusion.83
  135.7 51.2 %all-gather.5.cloned.1.call-done = bf16[4096,256]{0,1:T(8,128)(2,1)} async-done(((bf16[128,256]{0,1:T(8,128)(2,1)}), bf16[4096,256]{0,1:T(8,128)(2,1)}) %all-gather.5.cloned.1.call-update) | async-done | bytes 2097168 | tf_op jit(solution)/shard_map/all_gather | solution.py:35
  186.9 2.7 fusion.88
  189.6 2.3 copy.80
  191.9 1.3 copy.81
  193.3 13.4 %while.15 = (s32[]{:T(128)}, f32[1,4,128]{2,1,0:T(4,128)S(1)}, f32[1,4,128]{2,1,0:T(4,128)S(1)}, f32[1,4,128,128]{3,2,1,0:T(8,128)S(1)}, s32[8]{0:T(128)S(1)}, /...) while((s32[]{:T(128)}, f32[1,4,128]{2,1,0:T(4,128)S(1)}, ...), condition=%wide.region_8.9_spmd.clone, body=%wide.region_3.8_spmd.clone.sunk | while | flops 136775808 | bytes 4365611 | solution.py:192
  194.5 3.0 conditional.3
  194.7 1.2 fusion.87
  196.2 1.4 fusion.4
  206.8 1.3 convolution_convert_fusion
  208.1 6.7 %all-to-all-start = ((bf16[8,16,2048]{2,1,0:T(8,128)(2,1)}), bf16[8,16,2048]{2,1,0:T(8,128)(2,1)S(1)}, u32[]{:S(2)}, u32[]{:S(2)}) async-start(bf16[8,16,2048]{2,1,0:T(8,128)(2,1)} %bitcast.29), calls=%async_computation | async-start | bytes 1048576 | tf_op jit(solution)/shard_map/all_to_all | solution.py:46
  215.3 1.0 scatter_custom_fusion
  216.3 7.8 %all-to-all-done = bf16[8,16,2048]{2,1,0:T(8,128)(2,1)S(1)} async-done(((bf16[8,16,2048]{2,1,0:T(8,128)(2,1)}), bf16[8,16,2048]{2,1,0:T(8,128)(2,1)S(1)}, u32[]{:S(2)}, u32[]{:S(2)}) %all-to-all-start) | async-done | bytes 524320 | tf_op jit(solution)/shard_map/all_to_all | solution.py:46
  224.2 1.0 fusion.56
  225.3 1.4 gather_fusion
  226.7 0.7 reshape.607
  227.4 1.1 copy.70
  228.5 52.1 %all_to_all.23 = bf16[1,4,32,2,2048]{4,3,1,0,2:T(2,128)(2,1)S(1)} all-to-all(bf16[1,4,32,2,2048]{4,3,1,0,2:T(2,128)(2,1)S(1)} %copy.70), channel_id=1, replica_groups=mesh['sec'=32,'narrow_0'=4,'narrow_1'=2] {'sec'}, dimensions={2} | all-to-all | bytes 2097152 | tf_op jit(solution)/shard_map/all_to_all | solution.py:229
  280.6 0.8 copy.71
  281.4 5.7 stack.2
  287.1 102.8 %all_to_all.24 = bf16[8,1,4,32,2,2048]{5,4,3,2,1,0:T(2,128)(2,1)} all-to-all(bf16[8,1,4,32,2,2048]{5,4,3,2,1,0:T(2,128)(2,1)S(1)} %stack.2), channel_id=1, replica_groups=mesh['sec'=32,'narrow_0'=4,'narrow_1'=2] {'narrow_0','narrow_1'}, dimensions={0} | all-to-all | bytes 16777216 | tf_op jit(solution)/shard_map/all_to_all | solution.py:232
  389.9 13.2 %reshape.641 = bf16[8,4,64,2048]{3,2,1,0:T(8,128)(2,1)} reshape(bf16[8,1,4,32,2,2048]{5,4,3,2,1,0:T(2,128)(2,1)} %all_to_all.24) | data formatting | bytes 16777216 | tf_op jit(solution)/shard_map/reshape;reshape | solution.py:235
  403.1 5.7 fusion.28
  408.8 12.0 %convert_bitcast_fusion = bf16[8,4,64,2048]{3,2,0,1:T(8,128)(2,1)} fusion(bf16[4,96,2048]{2,1,0:T(8,128)(2,1)} %param.31, bf16[4,2048,96]{1,2,0:T(8,128)(2,1)} %param.30, bf16[8,4,64,2048]{3,2,1,0:T(8,128)(2,1)} %reshape.641, f32[8,4,64,96]{3,2,0,1:T(8,128)S(1)} %fusion.28), kind=kOutput, calls=%fused_computation.31 | convolution fusion | flops 1615986688 | bytes 20709376 | tf_op jit(solution)/shard_map/berf,efd->berd/dot_general | solution.py:241
  420.8 8.3 %copy.73 = bf16[8,4,64,2048]{3,2,1,0:T(8,128)(2,1)} copy(bf16[8,4,64,2048]{3,2,0,1:T(8,128)(2,1)} %convert_bitcast_fusion) | data formatting | bytes 16777216 | tf_op jit(solution)/shard_map/convert_element_type | solution.py:51
  429.2 78.5 %reduce-scatter.3.cloned.1.call-done = bf16[512,2048]{1,0:T(8,128)(2,1)} async-done(((bf16[2048,2048]{1,0:T(8,128)(2,1)}), bf16[512,2048]{1,0:T(8,128)(2,1)}) %reduce-scatter.3.cloned.1.call-update) | async-done | bytes 2097168 | tf_op jit(solution)/shard_map/reduce_scatter | solution.py:53
  507.7 37.9 %reduce-scatter.5.cloned.1.call-done = bf16[256,2048]{1,0:T(8,128)(2,1)} async-done(((bf16[512,2048]{1,0:T(8,128)(2,1)}), bf16[256,2048]{1,0:T(8,128)(2,1)}) %reduce-scatter.5.cloned.1.call-update) | async-done | bytes 1048592 | tf_op jit(solution)/shard_map/reduce_scatter | solution.py:53
  545.6 1.7 reshape.608
  547.4 2.1 copy.74
  549.5 10.1 %all-to-all-start.3 = ((bf16[1,4,32,2,2048]{4,3,1,0,2:T(2,128)(2,1)}), bf16[1,4,32,2,2048]{4,3,1,0,2:T(2,128)(2,1)S(1)}, u32[]{:S(2)}, u32[]{:S(2)}) async-start(bf16[1,4,32,2,2048]{4,3,1,0,2:T(2,128)(2,1)} %copy.74), calls=%async_computation.5 | async-start | bytes 2097152 | tf_op jit(solution)/shard_map/all_to_all | solution.py:246
  559.8 29.6 %all-to-all-done.3 = bf16[1,4,32,2,2048]{4,3,1,0,2:T(2,128)(2,1)S(1)} async-done(((bf16[1,4,32,2,2048]{4,3,1,0,2:T(2,128)(2,1)}), bf16[1,4,32,2,2048]{4,3,1,0,2:T(2,128)(2,1)S(1)}, u32[]{:S(2)}, u32[]{:S(2)}) %all-to-all-start.3) | async-done | bytes 1048608 | tf_op jit(solution)/shard_map/all_to_all | solution.py:246
  589.4 1.8 copy.75
  591.2 1.6 reshape.609
  592.8 1.7 gather_fusion.1
  594.6 1.5 fusion.51
  596.1 0.6 fusion.59
  (95 shorter events, 8.2 us)
Async XLA Ops:
  6.5 200.3 %copy-start = (bf16[512,2048]{1,0:T(8,128)(2,1)S(1)}, bf16[512,2048]{1,0:T(8,128)(2,1)}, u32[]{:S(2)}) copy-start(bf16[512,2048]{1,0:T(8,128)(2,1)} %param.25) | copy-start | bytes 6291460
  6.5 97.3 %all-gather.3.cloned.1.call-start = ((), (), s32[]{:S(2)}) async-start(), calls=%async_computation.6 | async-start | bytes 4718592 | tf_op jit(solution)/shard_map/all_gather | solution.py:21
  8.6 178.4 %all-gather.5.cloned.1.call-start = ((), (), s32[]{:S(2)}) async-start(), calls=%async_computation.7 | async-start | bytes 2162688 | tf_op jit(solution)/shard_map/all_gather | solution.py:35
  116.9 8.9 %copy-start.3 = (f32[2048]{0:T(1024)S(1)}, f32[2048]{0:T(1024)}, u32[]{:S(2)}) copy-start(f32[2048]{0:T(1024)} %param.19) | copy-start | bytes 24580
  125.8 5.1 copy-start.6
  125.8 6.1 %copy-start.5 = (s32[128,8]{0,1:T(8,128)S(1)}, s32[128,8]{0,1:T(8,128)}, u32[]{:S(2)}) copy-start(s32[128,8]{0,1:T(8,128)} %param.27) | copy-start | bytes 12292
  131.3 4.0 copy-start.7
  206.8 18.4 %copy-start.4 = (f32[2048]{0:T(1024)S(1)}, f32[2048]{0:T(1024)}, u32[]{:S(2)}) copy-start(f32[2048]{0:T(1024)} %param.26) | copy-start | bytes 24580
  208.1 16.0 %all-to-all-start = ((bf16[8,16,2048]{2,1,0:T(8,128)(2,1)}), bf16[8,16,2048]{2,1,0:T(8,128)(2,1)S(1)}, u32[]{:S(2)}, u32[]{:S(2)}) async-start(bf16[8,16,2048]{2,1,0:T(8,128)(2,1)} %bitcast.29), calls=%async_computation | async-start | bytes 1048576 | tf_op jit(solution)/shard_map/all_to_all | solution.py:46
  214.8 292.8 %reduce-scatter.3.cloned.1.call-start = ((), (), s32[]{:S(2)}) async-start(), calls=%async_computation.8 | async-start | bytes 10485760 | tf_op jit(solution)/shard_map/reduce_scatter | solution.py:53
  389.9 13.2 %copy-start.8 = (bf16[4,2048,96]{1,2,0:T(8,128)(2,1)S(1)}, bf16[4,2048,96]{1,2,0:T(8,128)(2,1)}, u32[]{:S(2)}) copy-start(bf16[4,2048,96]{1,2,0:T(8,128)(2,1)} %param.29) | copy-start | bytes 4718596
  429.1 116.5 %reduce-scatter.5.cloned.1.call-start = ((), (), s32[]{:S(2)}) async-start(), calls=%async_computation.9 | async-start | bytes 3145728 | tf_op jit(solution)/shard_map/reduce_scatter | solution.py:53
  547.3 12.2 %copy-start.2 = (f32[128,8]{0,1:T(8,128)S(1)}, f32[128,8]{0,1:T(8,128)}, u32[]{:S(2)}) copy-start(f32[128,8]{0,1:T(8,128)} %param.28) | copy-start | bytes 12292
  549.5 39.9 %all-to-all-start.3 = ((bf16[1,4,32,2,2048]{4,3,1,0,2:T(2,128)(2,1)}), bf16[1,4,32,2,2048]{4,3,1,0,2:T(2,128)(2,1)S(1)}, u32[]{:S(2)}, u32[]{:S(2)}) async-start(bf16[1,4,32,2,2048]{4,3,1,0,2:T(2,128)(2,1)} %copy.74), calls=%async_computation.5 | async-start | bytes 2097152 | tf_op jit(solution)/shard_map/all_to_all | solution.py:246
  591.2 5.5 copy-start.1
Sparse Core Ops, SparseCore 0:
  9.1 94.7 all-gather.2
  132.1 54.8 all-gather.4
  429.3 78.3 reduce-scatter.2
  510.0 35.5 reduce-scatter.4
